TPU v7x, 256 devices: a whole 4x4x8 slice. The times are simulated.
256 devices in a mesh: row: 32 (over y, z), col: 8 (over x, core).
Axes of the slice: x: 4, y: 4, z: 8, core: 2. Of those that a mesh axis runs over, the one named last changes fastest.
Arguments:
- tail_factor: bfloat16 [131072, 1024], P('row'), may hold values from -0.015625 to 0.015625
- tail_solution: bfloat16 [131072, 2048], P('row', 'col'), may hold values from -6 to 6
- panel_rhs: float32 [1024, 2048], P('row', 'col'), may hold values from -6 to 6
- panel_factor: bfloat16 [3, 512, 512], P(None, 'col'), as said below
Outputs:
- panel_solution: float32 [1024, 2048], P(None, 'col')
Inputs may be any that keep to these rules, and one draw needn't show every extreme that they name: panel_factor[0] and panel_factor[1] are unit lower triangular: ones on the diagonal and zeros above it.
All inputs are finite; a program needn't handle non-finite values.
Results may differ from a plain program's by a relative error of at most 0.0003.
Values may be sent and summed in bfloat16 or wider, within the bound.
A program may use at most 64 MiB of HBM per device.

v0:
```python
import jax
import jax.numpy as jnp
from jax import lax
from jax.sharding import PartitionSpec as P


def solve_block(lower, rhs):
    return jax.scipy.linalg.solve_triangular(lower, rhs, trans=1, lower=True, unit_diagonal=True)


def local_update(tail_factor, tail_solution):
    return lax.dot_general(
        tail_factor, tail_solution, (((0,), (0,)), ((), ())), preferred_element_type=jnp.float32
    )


def shards(tail_factor, tail_solution, panel_rhs, panel_factor):
    blocks = lax.all_gather(panel_factor, "col", axis=1, tiled=True).astype(jnp.float32)
    panel_width = tail_factor.shape[1]
    half_width = panel_width // 2
    whole_rhs = lax.all_gather(panel_rhs, "row", axis=0, tiled=True)
    term = local_update(tail_factor, tail_solution)
    summed = lax.psum(term, "row")
    reduced = whole_rhs - summed
    later = solve_block(blocks[1], reduced[half_width:])
    earlier_rhs = reduced[:half_width]
    adjusted = earlier_rhs - jnp.dot(
        blocks[2].T, later, precision=lax.Precision.HIGHEST, preferred_element_type=jnp.float32
    )
    earlier = solve_block(blocks[0], adjusted)
    return jnp.concatenate([earlier, later], axis=0)


def solution(mesh):
    return jax.shard_map(
        shards,
        mesh=mesh,
        in_specs=(P("row", None), P("row", "col"), P("row", "col"), P(None, "col", None)),
        out_specs=P(None, "col"),
        check_vma=False,
    )
```

profile of v0, /device:TPU:1, one launch (start us, length us, event | category | flops | bytes accessed | tf_op | source)
XLA Modules:
  0.0 406.2 jit_solution(5566970083653288185)
XLA Ops:
  6.5 1.6 copy-done
  8.1 6.7 %fusion.49 = f32[1024,256]{1,0:T(8,128)} fusion(bf16[4096,1024]{1,0:T(8,128)(2,1)} %param.6, bf16[4096,256]{1,0:T(8,128)(2,1)S(1)} %copy-done), kind=kOutput, calls=%fused_computation.78 | convolution fusion | flops 2147483648 | bytes 11534336 | tf_op jit(solution)/shard_map/dot_general | solution.py:12
  14.9 0.7 all-gather.5.cloned.1.call-update
  15.8 0.5 all-gather.3.cloned.1.call-update
  16.4 148.2 %all-reduce.2.cloned.1.call-done = f32[1024,256]{1,0:T(8,128)} async-done(((f32[1024,256]{1,0:T(8,128)}), f32[1024,256]{1,0:T(8,128)}) %all-reduce.2.cloned.1.call-update) | async-done | bytes 1048592 | tf_op jit(solution)/shard_map/psum | solution.py:23
  164.5 75.9 %all-gather.5.cloned.1.call-done = f32[1024,256]{1,0:T(8,128)} async-done(((f32[32,256]{1,0:T(8,128)}), f32[1024,256]{1,0:T(8,128)}) %all-gather.5.cloned.1.call-update) | async-done | bytes 1048592 | tf_op jit(solution)/shard_map/all_gather | solution.py:21
  240.5 1.7 sub.6
  242.1 30.1 %all-gather.3.cloned.1.call-done = bf16[3,512,512]{2,1,0:T(8,128)(2,1)} async-done(((bf16[3,64,512]{2,1,0:T(8,128)(2,1)}), bf16[3,512,512]{2,1,0:T(8,128)(2,1)}) %all-gather.3.cloned.1.call-update) | async-done | bytes 1572880 | tf_op jit(solution)/shard_map/all_gather | solution.py:18
  272.2 1.8 convert_element_type.3
  274.0 1.6 convert_add_fusion.1
  275.6 11.3 %while.4 = (s32[]{:T(128)}, f32[512,512]{1,0:T(8,128)}, s32[4,2]{0,1:T(2,128)S(1)}, f32[4,128,128]{2,1,0:T(8,128)S(1)}, s32[]{:T(128)}) while((s32[]{:T(128)}, f32[512,512]{1,0:T(8,128)}, s32[4,2]{0,1:T(2,128)S(1)}, f32[4,128,128]{2,1,0:T(8,128)S(1)}, s32[]{:T(128)}) %tuple.36), condition=%wide.while_cond, body=%wide.while_body.sunk | while | flops 2 | bytes 131181 | solution.py:8
  275.7 0.6 fusion.62
  276.3 2.2 bitcast_dynamic-update-slice_fusion.4
  278.6 0.6 fusion.62
  279.1 2.2 bitcast_dynamic-update-slice_fusion.4
  281.4 0.6 fusion.62
  282.0 2.2 bitcast_dynamic-update-slice_fusion.4
  284.2 0.6 fusion.62
  284.8 2.1 bitcast_dynamic-update-slice_fusion.4
  287.0 0.7 copy-done.4
  287.7 40.1 %custom-call.4 = f32[4,128,128]{1,2,0:T(8,128)S(1)} custom-call(f32[4,128,128]{2,1,0:T(8,128)} %copy-done.4), custom_call_target="InvertDiagBlocksLowerTriangular" | custom-call | tf_op jit(solution)/shard_map/jit(_solve_triangular)/triangular_solve | solution.py:8
  327.8 0.3 fusion.31
  328.1 0.4 copy-done.3
  328.5 1.1 convolution_subtract_fusion.5
  329.7 1.1 fusion.38
  330.8 1.3 convolution_subtract_fusion.3
  332.1 1.1 fusion.39
  333.2 1.4 convolution_subtract_fusion.2
  334.6 1.8 fusion.40
  336.4 0.7 broadcast.35.clone.1
  337.1 13.8 %while.5 = (s32[]{:T(128)}, f32[512,512]{1,0:T(8,128)}, s32[4,2]{0,1:T(2,128)S(1)}, f32[4,128,128]{2,1,0:T(8,128)}, s32[]{:T(128)}) while((s32[]{:T(128)}, f32[512,512]{1,0:T(8,128)}, s32[4,2]{0,1:T(2,128)S(1)}, f32[4,128,128]{2,1,0:T(8,128)}, s32[]{:T(128)}) %tuple.48), condition=%wide.while_cond.clone, body=%wide.while_body.clone.sunk | while | flops 2 | bytes 132705 | solution.py:8
  337.2 0.6 fusion.63
  337.7 2.8 bitcast_dynamic-update-slice_fusion.5
  340.7 0.6 fusion.63
  341.2 2.9 bitcast_dynamic-update-slice_fusion.5
  344.1 0.6 fusion.63
  344.7 2.9 bitcast_dynamic-update-slice_fusion.5
  347.6 0.6 fusion.63
  348.2 2.8 bitcast_dynamic-update-slice_fusion.5
  350.9 40.7 %custom-call.5 = f32[4,128,128]{1,2,0:T(8,128)} custom-call(f32[4,128,128]{2,1,0:T(8,128)} %get-tuple-element.21), custom_call_target="InvertDiagBlocksLowerTriangular" | custom-call | tf_op jit(solution)/shard_map/jit(_solve_triangular)/triangular_solve | solution.py:8
  391.7 1.9 fusion
  393.6 0.3 fusion.28
  393.9 1.2 convolution_subtract_fusion.4
  395.0 0.3 fusion.35
  395.3 1.3 convolution_subtract_fusion.1
  396.9 1.4 convolution_subtract_fusion
  398.3 0.3 fusion.41
  398.6 1.0 maximum_maximum_fusion
  (24 shorter events, 1.2 us)
Async XLA Ops:
  6.5 1.6 copy-start
  6.5 158.0 %all-reduce.2.cloned.1.call-start = ((), (), s32[]{:S(2)}) async-start(), calls=%async_computation.2 | async-start | bytes 2097152 | tf_op jit(solution)/shard_map/psum | solution.py:23
  14.9 225.6 %all-gather.5.cloned.1.call-start = ((), (), s32[]{:S(2)}) async-start(), calls=%async_computation.1 | async-start | bytes 1081344 | tf_op jit(solution)/shard_map/all_gather | solution.py:21
  15.6 256.6 %all-gather.3.cloned.1.call-start = ((), (), s32[]{:S(2)}) async-start(), calls=%async_computation | async-start | bytes 1769472 | tf_op jit(solution)/shard_map/all_gather | solution.py:18
  286.9 0.7 copy-start.4
  327.8 0.7 copy-start.3
  391.7 1.9 copy-start.2
  393.6 5.0 %copy-start.1 = (f32[128,256]{1,0:T(8,128)S(1)}, f32[128,256]{1,0:T(8,128)}, u32[]{:S(2)}) copy-start(f32[128,256]{1,0:T(8,128)} %fusion.40) | copy-start | bytes 393220
Sparse Core Ops, SparseCore 0:
  15.0 149.5 all-reduce.1
  167.1 73.2 all-gather.4
  242.3 29.8 all-gather.2
where the time goes:
time: 407 us; the launch traced here: 406 us
  waiting for transfers between devices  255 us (63%)
  other arithmetic  87 us (21%)
  local copies, waits for them, and re-layouts  28.6 us (7%)
  matrix products  21.6 us (5%)
  between operations  13.3 us (3%)
    psum x1, waiting for transfers between devices, shards(): summed = lax.psum(term, 'row')  148 us
    another operation x5, other arithmetic, solve_block(): jax.scipy.linalg.solve_triangular(lower, rhs, trans=1, lower=True, unit_d...  82.4 us
    all_gather x1, waiting for transfers between devices, shards(): whole_rhs = lax.all_gather(panel_rhs, 'row', axis=0, tiled=True)  75.9 us
    all_gather x1, waiting for transfers between devices, shards(): lax.all_gather(panel_factor, 'col', axis=1, tiled=True).astype(jnp.float32)  30.1 us
    another operation x27, local copies, waits for them, and re-layouts, solve_block(): jax.scipy.linalg.solve_triangular(lower, rhs, trans=1, lower=True, unit_d...  25.8 us
    another operation x14, matrix products, solve_block(): jax.scipy.linalg.solve_triangular(lower, rhs, trans=1, lower=True, unit_d...  13 us
  transfers between devices with their start and end apart: 3, of which 3 were waited for; matrix products, arithmetic and copies ran while one was open for 0% of the time, Pallas kernels for 0%

commit v1 on v0

--- a/solution.py
+++ b/solution.py
@@ -20,7 +20,7 @@
     half_width = panel_width // 2
     whole_rhs = lax.all_gather(panel_rhs, "row", axis=0, tiled=True)
     term = local_update(tail_factor, tail_solution)
-    summed = lax.psum(term, "row")
+    summed = jnp.sum(lax.all_gather(term, "row"), axis=0)
     reduced = whole_rhs - summed
     later = solve_block(blocks[1], reduced[half_width:])
     earlier_rhs = reduced[:half_width]

time: 407 us -> 390 us (0.958)
  waiting for transfers between devices: 255 us -> 225 us
  other arithmetic: 87 us -> 99.6 us
    psum x1 -> x0, waiting for transfers between devices: 148 us -> none  [shards(): summed = lax.psum(term, 'row')]
    all_gather x0 -> x1, waiting for transfers between devices: none -> 124 us  [shards(): summed = jnp.sum(lax.all_gather(term, 'row'), axis=0)]
    reduce_sum x0 -> x1, other arithmetic: none -> 12.9 us  [shards(): summed = jnp.sum(lax.all_gather(term, 'row'), axis=0)]
    all_gather x1, waiting for transfers between devices: 75.9 us -> 70.2 us  [shards(): whole_rhs = lax.all_gather(panel_rhs, 'row', axis=0, tiled=True)]
  transfers between devices with their start and end apart: 3 -> 3, of which waited for: 3 -> 3; matrix products, arithmetic and copies ran while one was open for 0% -> 30% of each run, Pallas kernels for 0% -> 0%
where the time goes in v1:
time: 390 us; the launch traced here: 389 us
  waiting for transfers between devices  225 us (58%)
  other arithmetic  99.6 us (26%)
  local copies, waits for them, and re-layouts  30.6 us (8%)
  matrix products  19.5 us (5%)
  between operations  13.3 us (3%)
    all_gather x1, waiting for transfers between devices, shards(): summed = jnp.sum(lax.all_gather(term, 'row'), axis=0)  124 us
    another operation x5, other arithmetic, solve_block(): jax.scipy.linalg.solve_triangular(lower, rhs, trans=1, lower=True, unit_d...  82.5 us
    all_gather x1, waiting for transfers between devices, shards(): whole_rhs = lax.all_gather(panel_rhs, 'row', axis=0, tiled=True)  70.2 us
    all_gather x1, waiting for transfers between devices, shards(): lax.all_gather(panel_factor, 'col', axis=1, tiled=True).astype(jnp.float32)  30.2 us
    another operation x27, local copies, waits for them, and re-layouts, solve_block(): jax.scipy.linalg.solve_triangular(lower, rhs, trans=1, lower=True, unit_d...  25.8 us
    reduce_sum x1, other arithmetic, shards(): summed = jnp.sum(lax.all_gather(term, 'row'), axis=0)  12.9 us
    another operation x14, matrix products, solve_block(): jax.scipy.linalg.solve_triangular(lower, rhs, trans=1, lower=True, unit_d...  11.1 us
  transfers between devices with their start and end apart: 3, of which 3 were waited for; matrix products, arithmetic and copies ran while one was open for 30% of the time, Pallas kernels for 0%

profile of v1, /device:TPU:1, one launch (start us, length us, event | category | flops | bytes accessed | tf_op | source)
XLA Modules:
  0.0 388.7 jit_solution(2904191619950237336)
XLA Ops:
  6.5 0.7 all-gather.7.cloned.1.call-update
  7.3 0.7 all-gather.5.cloned.1.call-update
  8.1 6.7 %fusion.49 = f32[1024,256]{1,0:T(8,128)} fusion(bf16[4096,1024]{1,0:T(8,128)(2,1)} %param.6, bf16[4096,256]{1,0:T(8,128)(2,1)S(1)} %copy-done), kind=kOutput, calls=%fused_computation.78 | convolution fusion | flops 2147483648 | bytes 11534336 | tf_op jit(solution)/shard_map/dot_general | solution.py:12
  14.9 70.2 %all-gather.7.cloned.1.call-done = f32[1024,256]{1,0:T(8,128)} async-done(((f32[32,256]{1,0:T(8,128)}), f32[1024,256]{1,0:T(8,128)}) %all-gather.7.cloned.1.call-update) | async-done | bytes 1048592 | tf_op jit(solution)/shard_map/all_gather | solution.py:21
  85.0 1.6 copy.6
  86.6 30.2 %all-gather.5.cloned.1.call-done = bf16[3,512,512]{2,1,0:T(8,128)(2,1)} async-done(((bf16[3,64,512]{2,1,0:T(8,128)(2,1)}), bf16[3,512,512]{2,1,0:T(8,128)(2,1)}) %all-gather.5.cloned.1.call-update) | async-done | bytes 1572880 | tf_op jit(solution)/shard_map/all_gather | solution.py:18
  116.8 1.8 convert_element_type.3
  118.6 1.6 convert_add_fusion.1
  120.2 11.3 %while.4 = (s32[]{:T(128)}, f32[512,512]{1,0:T(8,128)}, s32[4,2]{0,1:T(2,128)S(1)}, f32[4,128,128]{2,1,0:T(8,128)S(1)}, s32[]{:T(128)}) while((s32[]{:T(128)}, f32[512,512]{1,0:T(8,128)}, s32[4,2]{0,1:T(2,128)S(1)}, f32[4,128,128]{2,1,0:T(8,128)S(1)}, s32[]{:T(128)}) %tuple.36), condition=%wide.while_cond, body=%wide.while_body.sunk | while | flops 2 | bytes 131189 | solution.py:8
  120.4 0.5 fusion.62
  121.0 2.2 bitcast_dynamic-update-slice_fusion.4
  123.2 0.5 fusion.62
  123.8 2.2 bitcast_dynamic-update-slice_fusion.4
  126.0 0.5 fusion.62
  126.6 2.2 bitcast_dynamic-update-slice_fusion.4
  128.8 0.5 fusion.62
  129.4 2.1 bitcast_dynamic-update-slice_fusion.4
  131.5 0.7 copy-done.2
  132.2 40.1 %custom-call.4 = f32[4,128,128]{1,2,0:T(8,128)S(1)} custom-call(f32[4,128,128]{2,1,0:T(8,128)} %copy-done.2), custom_call_target="InvertDiagBlocksLowerTriangular" | custom-call | tf_op jit(solution)/shard_map/jit(_solve_triangular)/triangular_solve | solution.py:8
  172.3 0.7 broadcast.35.clone.1
  173.1 14.0 %while.5 = (s32[]{:T(128)}, f32[512,512]{1,0:T(8,128)}, s32[4,2]{0,1:T(2,128)S(1)}, f32[4,128,128]{2,1,0:T(8,128)}, s32[]{:T(128)}) while((s32[]{:T(128)}, f32[512,512]{1,0:T(8,128)}, s32[4,2]{0,1:T(2,128)S(1)}, f32[4,128,128]{2,1,0:T(8,128)}, s32[]{:T(128)}) %tuple.48), condition=%wide.while_cond.clone, body=%wide.while_body.clone.sunk | while | flops 2 | bytes 132205 | solution.py:8
  173.1 0.5 fusion.63
  173.7 2.9 bitcast_dynamic-update-slice_fusion.5
  176.6 0.5 fusion.63
  177.2 2.9 bitcast_dynamic-update-slice_fusion.5
  180.2 0.5 fusion.63
  180.7 2.9 bitcast_dynamic-update-slice_fusion.5
  183.7 0.5 fusion.63
  184.2 2.8 bitcast_dynamic-update-slice_fusion.5
  187.0 40.8 %custom-call.5 = f32[4,128,128]{1,2,0:T(8,128)} custom-call(f32[4,128,128]{2,1,0:T(8,128)} %get-tuple-element.21), custom_call_target="InvertDiagBlocksLowerTriangular" | custom-call | tf_op jit(solution)/shard_map/jit(_solve_triangular)/triangular_solve | solution.py:8
  227.8 123.6 %all-gather.9.cloned.1.call-done = f32[32768,256]{1,0:T(8,128)} async-done(((f32[1024,256]{1,0:T(8,128)}), f32[32768,256]{1,0:T(8,128)}) %all-gather.9.cloned.1.call-update) | async-done | bytes 33554448 | tf_op jit(solution)/shard_map/all_gather | solution.py:23
  351.4 12.9 %reduce_sum.9 = f32[1024,256]{1,0:T(8,128)} reduce(f32[32,1024,256]{2,1,0:T(8,128)} %bitcast.74, f32[]{:T(128)} %constant.10.clone.1), dimensions={0}, to_apply=%region_0.0 | reduce | flops 8126464 | bytes 34603012 | tf_op jit(solution)/shard_map/reduce_sum | solution.py:23
  364.3 2.5 copy.7
  366.9 1.4 sub.6
  368.2 0.3 fusion.31
  368.5 1.2 convolution_subtract_fusion.5
  369.7 0.3 fusion.38
  370.0 1.5 convolution_subtract_fusion.3
  371.5 0.3 fusion.39
  371.8 1.7 convolution_subtract_fusion.2
  373.6 0.3 fusion.40
  373.8 1.7 fusion
  375.5 0.3 fusion.28
  375.8 1.2 convolution_subtract_fusion.4
  377.3 1.5 convolution_subtract_fusion.1
  378.8 0.3 fusion.36
  379.1 1.8 convolution_subtract_fusion
  381.1 1.0 maximum_maximum_fusion
  (23 shorter events, 1.3 us)
Async XLA Ops:
  6.5 1.6 copy-start
  6.5 78.5 %all-gather.7.cloned.1.call-start = ((), (), s32[]{:S(2)}) async-start(), calls=%async_computation.1 | async-start | bytes 1081344 | tf_op jit(solution)/shard_map/all_gather | solution.py:21
  7.3 109.5 %all-gather.5.cloned.1.call-start = ((), (), s32[]{:S(2)}) async-start(), calls=%async_computation | async-start | bytes 1769472 | tf_op jit(solution)/shard_map/all_gather | solution.py:18
  8.0 343.4 %all-gather.9.cloned.1.call-start = ((), (), s32[]{:S(2)}) async-start(), calls=%async_computation.2 | async-start | bytes 34603008 | tf_op jit(solution)/shard_map/all_gather | solution.py:23
  131.5 0.7 copy-start.2
  368.2 7.3 %copy-start.1 = (f32[4,128,128]{1,2,0:T(8,128)S(1)}, f32[4,128,128]{1,2,0:T(8,128)}, u32[]{:S(2)}) copy-start(f32[4,128,128]{1,2,0:T(8,128)} %custom-call.5) | copy-start | bytes 786436
Sparse Core Ops, SparseCore 0:
  9.9 75.0 all-gather.6
  86.9 29.8 all-gather.4
  119.4 232.0 all-gather.8
